TPU v7x, 32 devices: a whole 2x2x4 slice. The times are simulated.
32 devices in a mesh: ia: 4 (over z), ja: 4 (over x, core), aux: 2 (over y).
Axes of the slice: x: 2, y: 2, z: 4, core: 2. Of those that a mesh axis runs over, the one named last changes fastest.
Arguments:
- raw_integrals: bfloat16 [2048, 12, 512], P(('ia', 'ja', 'aux')), may hold values from -0.5 to 0.5
- metric_root: bfloat16 [2048, 2048], replicated, may hold values from -0.125 to 0.125
- eps_occ: float32 [12], replicated, may hold values from -2 to -0.3
- eps_vir: float32 [512], replicated, may hold values from 0.3 to 3
Outputs:
- gamma: float32 [2048, 12, 512], P('ja', 'ia', 'aux')
All inputs are finite; a program needn't handle non-finite values.
Results may differ from a plain program's by a relative error of at most 0.0022.
Values may be sent and summed in bfloat16 or wider, within the bound.
No kernel may reach another device: no remote copies, remote signals or barrier semaphores. Data moves between devices by JAX's collectives and lax.ppermute only.
A program may use at most 128 MiB of HBM per device.

v0:
```python
import jax
import jax.numpy as jnp
from jax import lax
from jax.sharding import PartitionSpec as P

OB = 3
V = 512


def apply_metric(metric_root, raw_rows):
    return lax.dot_general(
        metric_root, raw_rows, (((0,), (0,)), ((), ())), preferred_element_type=jnp.float32
    ).astype(jnp.bfloat16)


def body(raw_integrals, metric_root, eps_occ, eps_vir):
    ia_count = lax.axis_size("ia")
    aux_count = lax.axis_size("aux")
    row_index = lax.axis_index("ia")
    col_index = lax.axis_index("ja")
    aux_index = lax.axis_index("aux")
    pieces = raw_integrals.shape[0]
    aux_total = metric_root.shape[0]
    narrow = V // (ia_count * aux_count)
    half_width = V // aux_count
    by_block = raw_integrals.reshape(pieces, ia_count, OB, ia_count * aux_count, narrow)
    own_rows = by_block.transpose(1, 3, 0, 2, 4).reshape(
        ia_count * ia_count * aux_count, pieces, OB * narrow
    )
    by_column = raw_integrals.reshape(pieces, ia_count, OB, ia_count, aux_count, narrow)
    own_cols = by_column.transpose(3, 1, 4, 0, 2, 5).reshape(
        ia_count * ia_count * aux_count, pieces, OB * narrow
    )
    got_rows, got_cols = (
        lax.all_to_all(own_rows, ("ia", "ja", "aux"), split_axis=0, concat_axis=1, tiled=True),
        lax.all_to_all(own_cols, ("ia", "ja", "aux"), split_axis=0, concat_axis=1, tiled=True),
    )
    joined = jnp.concatenate([got_rows[0], got_cols[0]], axis=1)
    fitted = apply_metric(metric_root, joined)
    row_block = fitted[:, : OB * narrow].reshape(aux_total, OB, narrow)
    col_block = fitted[:, OB * narrow :].reshape(aux_total, OB, narrow)
    block_i = lax.all_gather(row_block, ("ja", "aux"), axis=2, tiled=True)
    block_j = lax.all_gather(col_block, ("ia", "aux"), axis=2, tiled=True)
    half_i = lax.dynamic_slice_in_dim(block_i, aux_index * half_width, half_width, 2)
    half_j = lax.dynamic_slice_in_dim(block_j, aux_index * half_width, half_width, 2)
    flat_i = block_i.reshape(aux_total, OB * V)
    flat_j = block_j.reshape(aux_total, OB * V)
    contract_aux = (((0,), (0,)), ((), ()))
    direct_part = lax.dot_general(
        half_i.reshape(aux_total, OB * half_width),
        flat_j,
        contract_aux,
        preferred_element_type=jnp.float32,
    )
    swap_part = lax.dot_general(
        flat_i,
        half_j.reshape(aux_total, OB * half_width),
        contract_aux,
        preferred_element_type=jnp.float32,
    )
    swap_part = swap_part.reshape(OB, V, OB, half_width).transpose(0, 3, 2, 1)
    energy_i = lax.dynamic_slice_in_dim(eps_occ, row_index * OB, OB, 0)
    energy_j = lax.dynamic_slice_in_dim(eps_occ, col_index * OB, OB, 0)
    energy_a = lax.dynamic_slice_in_dim(eps_vir, aux_index * half_width, half_width, 0)
    denominator = (
        energy_a[None, :, None, None]
        + eps_vir[None, None, None, :]
        - energy_i[:, None, None, None]
        - energy_j[None, None, :, None]
    )
    amplitude = (
        (2.0 * direct_part.reshape(OB, half_width, OB, V) - swap_part) / denominator
    ).astype(jnp.bfloat16)
    amplitude = amplitude.reshape(OB * half_width, OB * V)
    ja_count = lax.axis_size("ja")
    q_rows = aux_total // ja_count
    share = lax.psum_scatter(
        lax.dot_general(
            flat_j, amplitude, (((1,), (1,)), ((), ())), preferred_element_type=jnp.float32
        ),
        "ja",
        scatter_dimension=0,
        tiled=True,
    )
    return share.reshape(q_rows, OB, half_width)


def solution(mesh):
    in_specs = (P(("ia", "ja", "aux"), None, None), P(), P(), P())
    out_specs = P("ja", "ia", "aux")
    return jax.shard_map(body, mesh=mesh, in_specs=in_specs, out_specs=out_specs, check_vma=False)
```

profile of v0, /device:TPU:0, one launch (start us, length us, event | category | flops | bytes accessed | tf_op | source)
XLA Modules:
  0.0 321.8 jit_solution(5210032561810463520)
XLA Ops:
  6.5 3.6 %reshape.91 = bf16[64,4,3,4,2,64]{5,4,3,0,2,1:T(2,128)(2,1)S(1)} reshape(bf16[64,12,512]{2,0,1:T(8,128)(2,1)} %param.4) | data formatting | bytes 1572864 | tf_op jit(solution)/shard_map/reshape | solution.py:30
  10.1 1.8 copy.23
  11.9 1.6 copy.24
  13.5 7.5 %all-to-all-start.1 = ((bf16[32,64,192]{2,1,0:T(8,128)(2,1)}), bf16[32,64,192]{2,1,0:T(8,128)(2,1)}, u32[]{:S(2)}, u32[]{:S(2)}) async-start(bf16[32,64,192]{2,1,0:T(8,128)(2,1)} %copy.24), calls=%async_computation.1 | async-start | bytes 2097152 | tf_op jit(solution)/shard_map/all_to_all | solution.py:36
  20.9 0.0 all-gather.3.cloned.1.call-start
  21.0 2.5 reshape.89
  23.4 1.1 copy.21
  24.6 0.8 copy.22
  25.4 21.8 %all-to-all-done.1 = bf16[32,64,192]{2,1,0:T(8,128)(2,1)} async-done(((bf16[32,64,192]{2,1,0:T(8,128)(2,1)}), bf16[32,64,192]{2,1,0:T(8,128)(2,1)}, u32[]{:S(2)}, u32[]{:S(2)}) %all-to-all-start.1) | async-done | bytes 786464 | tf_op jit(solution)/shard_map/all_to_all | solution.py:36
  47.1 29.6 %all_to_all.8 = bf16[32,64,192]{2,1,0:T(8,128)(2,1)S(1)} all-to-all(bf16[32,64,192]{2,1,0:T(8,128)(2,1)S(1)} %copy.22), channel_id=1, replica_groups=mesh['ia'=4,'ja'=4,'aux'=2] {'ia','ja','aux'}, dimensions={0} | all-to-all | bytes 1572864 | tf_op jit(solution)/shard_map/all_to_all | solution.py:35
  76.7 7.3 %fusion.14 = bf16[2048,384]{0,1:T(8,128)(2,1)S(1)} fusion(bf16[2048,2048]{1,0:T(8,128)(2,1)} %param.5, bf16[2048,192]{1,0:T(8,128)(2,1)} %bitcast.5, bf16[2048,192]{1,0:T(8,128)(2,1)S(1)} %bitcast.80), kind=kOutput, calls=%fused_computation.12 | convolution fusion | flops 3225157632 | bytes 11534336 | tf_op jit(solution)/shard_map/dot_general | solution.py:11
  84.1 0.0 copy-start
  84.1 0.0 copy-start.1
  84.1 1.3 fusion.21
  85.4 0.0 all-gather.3.cloned.1.call-update
  85.4 0.0 all-gather.5.cloned.1.call-start
  85.5 0.7 all-gather.5.cloned.1.call-update
  86.2 0.2 reduce-scatter.2.cloned.1.call-start
  86.4 0.0 copy-done
  86.4 0.1 dynamic_slice.17
  86.5 0.0 copy-done.1
  86.5 0.1 fusion.22
  86.6 0.1 broadcast_add_fusion
  86.7 0.3 broadcast_subtract_fusion
  87.0 96.3 %all-gather.3.cloned.1.call-done = bf16[2048,3,512]{0,2,1:T(8,128)(2,1)} async-done(((bf16[2048,3,64]{0,2,1:T(8,128)(2,1)}), bf16[2048,3,512]{0,2,1:T(8,128)(2,1)}) %all-gather.3.cloned.1.call-update) | async-done | bytes 6291472 | tf_op jit(solution)/shard_map/all_gather | solution.py:43
  183.3 45.5 %all-gather.5.cloned.1.call-done = bf16[2048,3,512]{0,2,1:T(8,128)(2,1)} async-done(((bf16[2048,3,64]{0,2,1:T(8,128)(2,1)}), bf16[2048,3,512]{0,2,1:T(8,128)(2,1)}) %all-gather.5.cloned.1.call-update) | async-done | bytes 6291472 | tf_op jit(solution)/shard_map/all_gather | solution.py:42
  228.8 0.0 copy-start.2
  228.8 0.0 copy-start.3
  228.8 8.4 %fusion = f32[3,512,3,256]{1,3,2,0:T(8,128)S(1)} fusion(bf16[2048,3,512]{0,2,1:T(8,128)(2,1)} %all-gather.5.cloned.1.call-done, bf16[2048,3,512]{0,2,1:T(8,128)(2,1)} %all-gather.3.cloned.1.call-done, s32[]{:T(128)S(6)} %select_n.11), kind=kOutput, calls=%fused_computation | convolution fusion | flops 4831838208 | bytes 14155780 | tf_op jit(solution)/shard_map/dot_general | solution.py:55
  237.2 0.0 copy-done.2
  237.2 0.0 copy-done.3
  237.3 5.6 %fusion.5 = bf16[3,256,3,512]{3,1,2,0:T(8,128)(2,1)S(1)} fusion(f32[3,512,3,256]{1,3,2,0:T(8,128)S(1)} %fusion, bf16[2048,3,512]{0,2,1:T(8,128)(2,1)S(1)} %copy-done.2, bf16[2048,3,512]{0,2,1:T(8,128)(2,1)S(1)} %copy-done.3, s32[]{:T(128)S(6)} %select_n.11, f32[3]{0:T(128)S(1)} %get-tuple-element.8, f32[3,256,512]{2,1,0:T(8,128)S(1)} %broadcast_subtract_fusion), kind=kOutput, calls=%fused_computation.6 | convolution fusion | flops 4837736448 | bytes 18088452 | tf_op jit(solution)/shard_map/dot_general | solution.py:49
  242.9 2.0 copy.26
  244.9 0.8 copy.32
  245.7 7.1 %fusion.23 = f32[2048,768]{1,0:T(8,128)} fusion(bf16[2048,1536]{0,1:T(8,128)(2,1)S(1)} %bitcast.81, bf16[768,1536]{1,0:T(8,128)(2,1)S(1)} %bitcast.79), kind=kOutput, calls=%fused_computation.23 | convolution fusion | flops 4831838208 | bytes 14942208 | tf_op jit(solution)/shard_map/dot_general | solution.py:78
  252.8 0.0 reduce-scatter.2.cloned.1.call-update
  252.8 59.0 %reduce-scatter.2.cloned.1.call-done = f32[512,768]{1,0:T(8,128)} async-done(((f32[2048,768]{1,0:T(8,128)}), f32[512,768]{1,0:T(8,128)}) %reduce-scatter.2.cloned.1.call-update) | async-done | bytes 1572880 | tf_op jit(solution)/shard_map/reduce_scatter | solution.py:77
  311.8 1.9 copy.27
  313.7 1.6 copy.28
Async XLA Ops:
  13.5 33.6 %all-to-all-start.1 = ((bf16[32,64,192]{2,1,0:T(8,128)(2,1)}), bf16[32,64,192]{2,1,0:T(8,128)(2,1)}, u32[]{:S(2)}, u32[]{:S(2)}) async-start(bf16[32,64,192]{2,1,0:T(8,128)(2,1)} %copy.24), calls=%async_computation.1 | async-start | bytes 2097152 | tf_op jit(solution)/shard_map/all_to_all | solution.py:36
  20.9 162.4 %all-gather.3.cloned.1.call-start = ((), (), s32[]{:S(2)}) async-start(), calls=%async_computation.3 | async-start | bytes 7077888 | tf_op jit(solution)/shard_map/all_gather | solution.py:43
  84.1 2.4 copy-start
  84.1 2.4 copy-start.1
  85.4 143.4 %all-gather.5.cloned.1.call-start = ((), (), s32[]{:S(2)}) async-start(), calls=%async_computation.4 | async-start | bytes 7077888 | tf_op jit(solution)/shard_map/all_gather | solution.py:42
  86.2 225.6 %reduce-scatter.2.cloned.1.call-start = ((), (), s32[]{:S(2)}) async-start(), calls=%async_computation.5 | async-start | bytes 7864320 | tf_op jit(solution)/shard_map/reduce_scatter | solution.py:77
  228.8 8.4 %copy-start.2 = (bf16[2048,3,512]{0,2,1:T(8,128)(2,1)S(1)}, bf16[2048,3,512]{0,2,1:T(8,128)(2,1)}, u32[]{:S(2)}) copy-start(bf16[2048,3,512]{0,2,1:T(8,128)(2,1)} %all-gather.3.cloned.1.call-done) | copy-start | bytes 18874372
  228.8 8.4 %copy-start.3 = (bf16[2048,3,512]{0,2,1:T(8,128)(2,1)S(1)}, bf16[2048,3,512]{0,2,1:T(8,128)(2,1)}, u32[]{:S(2)}) copy-start(bf16[2048,3,512]{0,2,1:T(8,128)(2,1)} %all-gather.5.cloned.1.call-done) | copy-start | bytes 18874372
Sparse Core Ops, SparseCore 0:
  85.6 97.7 all-gather.2
  185.2 43.5 all-gather.4
  252.9 58.8 reduce-scatter.1
where the time goes:
time: 322 us
  waiting for transfers between devices  223 us (69%)
  blocking collectives  29.6 us (9%)
  matrix products  28.4 us (9%)
  local copies, waits for them, and re-layouts  19.1 us (6%)
  between operations  13.3 us (4%)
  starting transfers between devices  7.76 us (2%)
    all_gather x1, waiting for transfers between devices, body(): block_j = lax.all_gather(col_block, ('ia', 'aux'), axis=2, tiled=True)  96.3 us
    reduce_scatter x1, waiting for transfers between devices, body(): lax.psum_scatter(lax.dot_general(flat_j, amplitude, (((1,), (1,)), ((), (...  59 us
    all_gather x1, waiting for transfers between devices, body(): block_i = lax.all_gather(row_block, ('ja', 'aux'), axis=2, tiled=True)  45.5 us
    all_to_all x1, blocking collectives, body(): lax.all_to_all(own_rows, ('ia', 'ja', 'aux'), split_axis=0, concat_axis=1...  29.6 us
    all_to_all x1, waiting for transfers between devices, body(): lax.all_to_all(own_cols, ('ia', 'ja', 'aux'), split_axis=0, concat_axis=1...  21.8 us
    dot_general x1, matrix products, body(): lax.dot_general(flat_i, half_j.reshape(aux_total, OB * half_width), contr...  8.42 us
    all_to_all x1, starting transfers between devices, body(): lax.all_to_all(own_cols, ('ia', 'ja', 'aux'), split_axis=0, concat_axis=1...  7.45 us
    dot_general x1, matrix products, apply_metric(): lax.dot_general(metric_root, raw_rows, (((0,), (0,)), ((), ())), preferre...  7.32 us
  transfers between devices with their start and end apart: 4, of which 4 were waited for; matrix products, arithmetic and copies ran while one was open for 2% of the time, Pallas kernels for 0%

commit v1 on v0

--- a/solution.py
+++ b/solution.py
@@ -5,6 +5,27 @@
 
 OB = 3
 V = 512
+
+
+def collect(x, axis, dim):
+    size, index, rows = (lax.axis_size(axis), lax.axis_index(axis), x.shape[dim])
+    right = [(i, (i + 1) % size) for i in range(size)]
+    backward = [(i, (i - 1) % size) for i in range(size)]
+    out = jnp.zeros((*x.shape[:dim], size * rows, *x.shape[dim + 1 :]), x.dtype)
+    out = lax.dynamic_update_slice_in_dim(out, x, index * rows, axis=dim)
+    from_left = from_right = x
+    half = size // 2
+    for turn in range(1, half + 1):
+        from_left = lax.ppermute(from_left, axis, right)
+        out = lax.dynamic_update_slice_in_dim(
+            out, from_left, (index - turn) % size * rows, axis=dim
+        )
+        if turn < size - half:
+            from_right = lax.ppermute(from_right, axis, backward)
+            out = lax.dynamic_update_slice_in_dim(
+                out, from_right, (index + turn) % size * rows, axis=dim
+            )
+    return out
 
 
 def apply_metric(metric_root, raw_rows):
@@ -39,7 +60,7 @@
     fitted = apply_metric(metric_root, joined)
     row_block = fitted[:, : OB * narrow].reshape(aux_total, OB, narrow)
     col_block = fitted[:, OB * narrow :].reshape(aux_total, OB, narrow)
-    block_i = lax.all_gather(row_block, ("ja", "aux"), axis=2, tiled=True)
+    block_i = collect(row_block, ("ja", "aux"), 2)
     block_j = lax.all_gather(col_block, ("ia", "aux"), axis=2, tiled=True)
     half_i = lax.dynamic_slice_in_dim(block_i, aux_index * half_width, half_width, 2)
     half_j = lax.dynamic_slice_in_dim(block_j, aux_index * half_width, half_width, 2)

time: 322 us -> 346 us (1.075)
  starting transfers between devices: 7.76 us -> 67.2 us
  waiting for transfers between devices: 223 us -> 169 us
  local copies, waits for them, and re-layouts: 19.1 us -> 33.4 us
    all_gather x1, waiting for transfers between devices: 96.3 us -> 0.01 us  [body(): block_j = lax.all_gather(col_block, ('ia', 'aux'), axis=2, tiled=True)]
    ppermute x0 -> x7, waiting for transfers between devices: none -> 90.1 us  [the longest x3 48.3 us: collect(): from_right = lax.ppermute(from_right, axis, backward)]
    ppermute x0 -> x7, starting transfers between devices: none -> 59.6 us  [the longest x4 58.4 us: collect(): from_left = lax.ppermute(from_left, axis, right)]
    all_gather x1 -> x0, waiting for transfers between devices: 45.5 us -> none  [body(): block_i = lax.all_gather(row_block, ('ja', 'aux'), axis=2, tiled=True)]
    dynamic_update_slice x0 -> x8, local copies, waits for them, and re-layouts: none -> 11.3 us  [the longest x3 5.28 us: collect(): lax.dynamic_update_slice_in_dim(out, from_right, (index + turn) % size *...]
  transfers between devices with their start and end apart: 4 -> 10, of which waited for: 4 -> 7; matrix products, arithmetic and copies ran while one was open for 2% -> 6% of each run, Pallas kernels for 0% -> 0%
where the time goes in v1:
time: 346 us; the launch traced here: 345 us
  waiting for transfers between devices  169 us (49%)
  starting transfers between devices  67.2 us (19%)
  local copies, waits for them, and re-layouts  33.4 us (10%)
  matrix products  31.6 us (9%)
  blocking collectives  29.6 us (9%)
  between operations  13.7 us (4%)
    reduce_scatter x1, waiting for transfers between devices, body(): lax.psum_scatter(lax.dot_general(flat_j, amplitude, (((1,), (1,)), ((), (...  59.3 us
    ppermute x4, starting transfers between devices, collect(): from_left = lax.ppermute(from_left, axis, right)  58.4 us
    ppermute x3, waiting for transfers between devices, collect(): from_right = lax.ppermute(from_right, axis, backward)  48.3 us
    ppermute x4, waiting for transfers between devices, collect(): from_left = lax.ppermute(from_left, axis, right)  41.7 us
    all_to_all x1, blocking collectives, body(): lax.all_to_all(own_cols, ('ia', 'ja', 'aux'), split_axis=0, concat_axis=1...  29.6 us
    all_to_all x1, waiting for transfers between devices, body(): lax.all_to_all(own_rows, ('ia', 'ja', 'aux'), split_axis=0, concat_axis=1...  20 us
    dot_general x1, matrix products, body(): lax.dot_general(flat_i, half_j.reshape(aux_total, OB * half_width), contr...  8.86 us
    dot_general x1, matrix products, body(): lax.dot_general(half_i.reshape(aux_total, OB * half_width), flat_j, contr...  8.36 us
  transfers between devices with their start and end apart: 10, of which 7 were waited for; matrix products, arithmetic and copies ran while one was open for 6% of the time, Pallas kernels for 0%

profile of v1, /device:TPU:0, one launch (start us, length us, event | category | flops | bytes accessed | tf_op | source)
XLA Modules:
  0.0 345.2 jit_solution(15624809855511488891)
XLA Ops:
  6.5 2.4 reshape.89
  9.0 1.1 copy.21
  10.1 1.6 copy.22
  11.7 7.5 %all-to-all-start = ((bf16[32,64,192]{2,1,0:T(8,128)(2,1)}), bf16[32,64,192]{2,1,0:T(8,128)(2,1)}, u32[]{:S(2)}, u32[]{:S(2)}) async-start(bf16[32,64,192]{2,1,0:T(8,128)(2,1)} %copy.22), calls=%async_computation | async-start | bytes 2097152 | tf_op jit(solution)/shard_map/all_to_all | solution.py:56
  19.1 0.0 all-gather.2.cloned.1.call-start
  19.2 3.6 %reshape.91 = bf16[64,4,3,4,2,64]{5,4,3,0,2,1:T(2,128)(2,1)S(1)} reshape(bf16[64,12,512]{2,0,1:T(8,128)(2,1)} %param.4) | data formatting | bytes 1572864 | tf_op jit(solution)/shard_map/reshape | solution.py:51
  22.8 1.8 copy.23
  24.6 0.8 copy.24
  25.4 20.0 %all-to-all-done = bf16[32,64,192]{2,1,0:T(8,128)(2,1)} async-done(((bf16[32,64,192]{2,1,0:T(8,128)(2,1)}), bf16[32,64,192]{2,1,0:T(8,128)(2,1)}, u32[]{:S(2)}, u32[]{:S(2)}) %all-to-all-start) | async-done | bytes 786464 | tf_op jit(solution)/shard_map/all_to_all | solution.py:56
  45.3 29.6 %all_to_all.8 = bf16[32,64,192]{2,1,0:T(8,128)(2,1)S(1)} all-to-all(bf16[32,64,192]{2,1,0:T(8,128)(2,1)S(1)} %copy.24), channel_id=1, replica_groups=mesh['ia'=4,'ja'=4,'aux'=2] {'ia','ja','aux'}, dimensions={0} | all-to-all | bytes 1572864 | tf_op jit(solution)/shard_map/all_to_all | solution.py:57
  74.9 7.3 %fusion.14 = bf16[2048,384]{0,1:T(8,128)(2,1)S(1)} fusion(bf16[2048,2048]{1,0:T(8,128)(2,1)} %param.5, bf16[2048,192]{1,0:T(8,128)(2,1)S(1)} %bitcast.82, bf16[2048,192]{1,0:T(8,128)(2,1)} %bitcast.2), kind=kOutput, calls=%fused_computation.12 | convolution fusion | flops 3225157632 | bytes 11534336 | tf_op jit(solution)/shard_map/dot_general | solution.py:32
  82.3 1.0 fusion.21
  83.3 0.0 all-gather.2.cloned.1.call-update
  83.3 0.0 reduce-scatter.2.cloned.1.call-start
  83.4 1.5 collective-permute-start
  84.9 1.2 collective-permute-start.1
  86.1 33.6 %collective-permute-done = bf16[2048,3,64]{0,2,1:T(8,128)(2,1)S(1)} collective-permute-done((bf16[2048,3,64]{0,2,1:T(8,128)(2,1)S(1)}, bf16[2048,3,64]{0,2,1:T(8,128)(2,1)S(1)}, u32[]{:S(2)}, u32[]{:S(2)}) %collective-permute-start) | collective-permute-done | bytes 786464 | tf_op jit(solution)/shard_map/ppermute | solution.py:19
  119.7 2.5 collective-permute-start.2
  122.2 0.1 dynamic_slice.17
  122.3 0.1 broadcast_add_fusion
  122.4 27.7 %collective-permute-done.1 = bf16[2048,3,64]{0,2,1:T(8,128)(2,1)} collective-permute-done((bf16[2048,3,64]{0,2,1:T(8,128)(2,1)S(1)}, bf16[2048,3,64]{0,2,1:T(8,128)(2,1)}, u32[]{:S(2)}, u32[]{:S(2)}) %collective-permute-start.1) | collective-permute-done | bytes 786464 | tf_op jit(solution)/shard_map/ppermute | solution.py:24
  150.1 0.0 collective-permute-start.3
  150.1 0.1 fusion.22
  150.2 0.0 collective-permute-done.2
  150.2 37.1 %collective-permute-start.4 = (bf16[2048,3,64]{0,2,1:T(8,128)(2,1)S(1)}, bf16[2048,3,64]{0,2,1:T(8,128)(2,1)}, u32[]{:S(2)}, u32[]{:S(2)}) collective-permute-start(bf16[2048,3,64]{0,2,1:T(8,128)(2,1)S(1)} %collective-permute-done.2), channel_id=1, source_target_pairs={{0,1},{1,2},{2,3},{3,4},{4,5},{5,6},{6,7},{7,0},{8,9},{9,10},{10,1... | collective-permute-start | bytes 2359304 | tf_op jit(solution)/shard_map/ppermute | solution.py:19
  187.3 0.3 broadcast_subtract_fusion
  187.7 3.4 broadcast_in_dim.2
  191.1 1.0 constant_dynamic-update-slice_fusion.7
  192.1 0.9 constant_dynamic-update-slice_fusion.6
  193.0 17.0 %collective-permute-done.3 = bf16[2048,3,64]{0,2,1:T(8,128)(2,1)} collective-permute-done((bf16[2048,3,64]{0,2,1:T(8,128)(2,1)}, bf16[2048,3,64]{0,2,1:T(8,128)(2,1)}, u32[]{:S(2)}, u32[]{:S(2)}) %collective-permute-start.3) | collective-permute-done | bytes 786464 | tf_op jit(solution)/shard_map/ppermute | solution.py:24
  210.0 2.2 constant_dynamic-update-slice_fusion.5
  212.2 17.3 %collective-permute-start.6 = (bf16[2048,3,64]{0,2,1:T(8,128)(2,1)}, bf16[2048,3,64]{0,2,1:T(8,128)(2,1)S(1)}, u32[]{:S(2)}, u32[]{:S(2)}) collective-permute-start(bf16[2048,3,64]{0,2,1:T(8,128)(2,1)} %collective-permute-done.4), channel_id=1, source_target_pairs={{0,1},{1,2},{2,3},{3,4},{4,5},{5,6},{6,7},{7,0},{8,9},{9,10},{10,1... | collective-permute-start | bytes 2359304 | tf_op jit(solution)/shard_map/ppermute | solution.py:19
  229.5 1.0 constant_dynamic-update-slice_fusion.4
  230.5 2.1 constant_dynamic-update-slice_fusion.3
  232.6 2.1 constant_dynamic-update-slice_fusion.2
  234.8 3.6 %collective-permute-done.5 = bf16[2048,3,64]{0,2,1:T(8,128)(2,1)S(1)} collective-permute-done((bf16[2048,3,64]{0,2,1:T(8,128)(2,1)}, bf16[2048,3,64]{0,2,1:T(8,128)(2,1)S(1)}, u32[]{:S(2)}, u32[]{:S(2)}) %collective-permute-start.5) | collective-permute-done | bytes 786464 | tf_op jit(solution)/shard_map/ppermute | solution.py:24
  238.4 0.9 constant_dynamic-update-slice_fusion.1
  239.4 8.1 %collective-permute-done.6 = bf16[2048,3,64]{0,2,1:T(8,128)(2,1)S(1)} collective-permute-done((bf16[2048,3,64]{0,2,1:T(8,128)(2,1)}, bf16[2048,3,64]{0,2,1:T(8,128)(2,1)S(1)}, u32[]{:S(2)}, u32[]{:S(2)}) %collective-permute-start.6) | collective-permute-done | bytes 786464 | tf_op jit(solution)/shard_map/ppermute | solution.py:19
  247.5 1.0 constant_dynamic-update-slice_fusion
  248.5 8.4 %fusion.2 = f32[3,256,3,512]{3,1,2,0:T(8,128)S(1)} fusion(bf16[2048,3,512]{0,2,1:T(8,128)(2,1)} %all-gather.2.cloned.1.call-done, bf16[2048,3,512]{0,2,1:T(8,128)(2,1)} %constant_dynamic-update-slice_fusion, s32[]{:T(128)S(6)} %select_n.81), kind=kOutput, calls=%fused_computation.2 | convolution fusion | flops 4831838208 | bytes 14155780 | tf_op jit(solution)/shard_map/dot_general | solution.py:70
  256.8 8.9 %fusion.5 = bf16[3,256,3,512]{3,1,2,0:T(8,128)(2,1)S(1)} fusion(f32[3,256,3,512]{3,1,2,0:T(8,128)S(1)} %fusion.2, bf16[2048,3,512]{0,2,1:T(8,128)(2,1)S(1)} %copy-done.4, s32[]{:T(128)S(6)} %select_n.81, bf16[2048,3,512]{0,2,1:T(8,128)(2,1)} %constant_dynamic-update-slice_fusion, f32[3]{0:T(128)S(1)} %get-tuple-element.8, ...), kind=kOutput, calls=%fused_computation.6 | convolution fusion | flops 4837736448 | bytes 18088452 | tf_op jit(solution)/shard_map/dot_general | solution.py:76
  265.7 2.0 copy.26
  267.7 0.8 copy.32
  268.5 7.1 %fusion.23 = f32[2048,768]{1,0:T(8,128)} fusion(bf16[2048,1536]{0,1:T(8,128)(2,1)S(1)} %bitcast.83, bf16[768,1536]{1,0:T(8,128)(2,1)S(1)} %bitcast.81), kind=kOutput, calls=%fused_computation.31 | convolution fusion | flops 4831838208 | bytes 14942208 | tf_op jit(solution)/shard_map/dot_general | solution.py:99
  275.6 0.0 reduce-scatter.2.cloned.1.call-update
  275.6 59.3 %reduce-scatter.2.cloned.1.call-done = f32[512,768]{1,0:T(8,128)} async-done(((f32[2048,768]{1,0:T(8,128)}), f32[512,768]{1,0:T(8,128)}) %reduce-scatter.2.cloned.1.call-update) | async-done | bytes 1572880 | tf_op jit(solution)/shard_map/reduce_scatter | solution.py:98
  334.9 1.9 copy.27
  336.8 1.6 copy.28
  (13 shorter events, 0.0 us)
Async XLA Ops:
  11.7 33.6 %all-to-all-start = ((bf16[32,64,192]{2,1,0:T(8,128)(2,1)}), bf16[32,64,192]{2,1,0:T(8,128)(2,1)}, u32[]{:S(2)}, u32[]{:S(2)}) async-start(bf16[32,64,192]{2,1,0:T(8,128)(2,1)} %copy.22), calls=%async_computation | async-start | bytes 2097152 | tf_op jit(solution)/shard_map/all_to_all | solution.py:56
  19.1 229.3 %all-gather.2.cloned.1.call-start = ((), (), s32[]{:S(2)}) async-start(), calls=%async_computation.3 | async-start | bytes 7077888 | tf_op jit(solution)/shard_map/all_gather | solution.py:64
  74.9 47.3 %copy-start.2 = (f32[512]{0:T(512)S(1)}, f32[512]{0:T(512)}, u32[]{:S(2)}) copy-start(f32[512]{0:T(512)} %param.7) | copy-start | bytes 6148
  74.9 75.1 %copy-start.3 = (f32[12]{0:T(128)S(1)}, f32[12]{0:T(128)}, u32[]{:S(2)}) copy-start(f32[12]{0:T(128)} %param.6) | copy-start | bytes 148
  83.3 251.6 %reduce-scatter.2.cloned.1.call-start = ((), (), s32[]{:S(2)}) async-start(), calls=%async_computation.4 | async-start | bytes 7864320 | tf_op jit(solution)/shard_map/reduce_scatter | solution.py:98
  83.4 36.3 %collective-permute-start = (bf16[2048,3,64]{0,2,1:T(8,128)(2,1)S(1)}, bf16[2048,3,64]{0,2,1:T(8,128)(2,1)S(1)}, u32[]{:S(2)}, u32[]{:S(2)}) collective-permute-start(bf16[2048,3,64]{0,2,1:T(8,128)(2,1)S(1)} %bitcast.78), channel_id=1, source_target_pairs={{0,1},{1,2},{2,3},{3,4},{4,5},{5,6},{6,7},{7,0},{8,9},{9,10},{10,1... | collective-permute-start | bytes 2359304 | tf_op jit(solution)/shard_map/ppermute | solution.py:19
  84.9 65.2 %collective-permute-start.1 = (bf16[2048,3,64]{0,2,1:T(8,128)(2,1)S(1)}, bf16[2048,3,64]{0,2,1:T(8,128)(2,1)}, u32[]{:S(2)}, u32[]{:S(2)}) collective-permute-start(bf16[2048,3,64]{0,2,1:T(8,128)(2,1)S(1)} %bitcast.79), channel_id=1, source_target_pairs={{0,7},{1,0},{2,1},{3,2},{4,3},{5,4},{6,5},{7,6},{8,15},{9,8},{10,9... | collective-permute-start | bytes 2359304 | tf_op jit(solution)/shard_map/ppermute | solution.py:24
  119.7 67.6 %copy-start = (bf16[2048,3,64]{0,2,1:T(8,128)(2,1)}, bf16[2048,3,64]{0,2,1:T(8,128)(2,1)S(1)}, u32[]{:S(2)}) copy-start(bf16[2048,3,64]{0,2,1:T(8,128)(2,1)S(1)} %collective-permute-done) | copy-start | bytes 2359300
  119.7 30.5 %collective-permute-start.2 = (bf16[2048,3,64]{0,2,1:T(8,128)(2,1)S(1)}, bf16[2048,3,64]{0,2,1:T(8,128)(2,1)S(1)}, u32[]{:S(2)}, u32[]{:S(2)}) collective-permute-start(bf16[2048,3,64]{0,2,1:T(8,128)(2,1)S(1)} %collective-permute-done), channel_id=1, source_target_pairs={{0,1},{1,2},{2,3},{3,4},{4,5},{5,6},{6,7},{7,0},{8,9},{9,10},{10,1... | collective-permute-start | bytes 2359304 | tf_op jit(solution)/shard_map/ppermute | solution.py:19
  150.1 59.9 %collective-permute-start.3 = (bf16[2048,3,64]{0,2,1:T(8,128)(2,1)}, bf16[2048,3,64]{0,2,1:T(8,128)(2,1)}, u32[]{:S(2)}, u32[]{:S(2)}) collective-permute-start(bf16[2048,3,64]{0,2,1:T(8,128)(2,1)} %collective-permute-done.1), channel_id=1, source_target_pairs={{0,7},{1,0},{2,1},{3,2},{4,3},{5,4},{6,5},{7,6},{8,15},{9,8},{10,9... | collective-permute-start | bytes 2359304 | tf_op jit(solution)/shard_map/ppermute | solution.py:24
  150.2 62.0 %collective-permute-start.4 = (bf16[2048,3,64]{0,2,1:T(8,128)(2,1)S(1)}, bf16[2048,3,64]{0,2,1:T(8,128)(2,1)}, u32[]{:S(2)}, u32[]{:S(2)}) collective-permute-start(bf16[2048,3,64]{0,2,1:T(8,128)(2,1)S(1)} %collective-permute-done.2), channel_id=1, source_target_pairs={{0,1},{1,2},{2,3},{3,4},{4,5},{5,6},{6,7},{7,0},{8,9},{9,10},{10,1... | collective-permute-start | bytes 2359304 | tf_op jit(solution)/shard_map/ppermute | solution.py:19
  187.7 4.4 %copy-start.1 = (bf16[2048,3,64]{0,2,1:T(8,128)(2,1)S(1)}, bf16[2048,3,64]{0,2,1:T(8,128)(2,1)}, u32[]{:S(2)}) copy-start(bf16[2048,3,64]{0,2,1:T(8,128)(2,1)} %copy-done) | copy-start | bytes 2359300
  210.0 28.4 %collective-permute-start.5 = (bf16[2048,3,64]{0,2,1:T(8,128)(2,1)}, bf16[2048,3,64]{0,2,1:T(8,128)(2,1)S(1)}, u32[]{:S(2)}, u32[]{:S(2)}) collective-permute-start(bf16[2048,3,64]{0,2,1:T(8,128)(2,1)} %collective-permute-done.3), channel_id=1, source_target_pairs={{0,7},{1,0},{2,1},{3,2},{4,3},{5,4},{6,5},{7,6},{8,15},{9,8},{10,9... | collective-permute-start | bytes 2359304 | tf_op jit(solution)/shard_map/ppermute | solution.py:24
  212.2 35.3 %collective-permute-start.6 = (bf16[2048,3,64]{0,2,1:T(8,128)(2,1)}, bf16[2048,3,64]{0,2,1:T(8,128)(2,1)S(1)}, u32[]{:S(2)}, u32[]{:S(2)}) collective-permute-start(bf16[2048,3,64]{0,2,1:T(8,128)(2,1)} %collective-permute-done.4), channel_id=1, source_target_pairs={{0,1},{1,2},{2,3},{3,4},{4,5},{5,6},{6,7},{7,0},{8,9},{9,10},{10,1... | collective-permute-start | bytes 2359304 | tf_op jit(solution)/shard_map/ppermute | solution.py:19
  248.4 8.4 %copy-start.4 = (bf16[2048,3,512]{0,2,1:T(8,128)(2,1)S(1)}, bf16[2048,3,512]{0,2,1:T(8,128)(2,1)}, u32[]{:S(2)}) copy-start(bf16[2048,3,512]{0,2,1:T(8,128)(2,1)} %all-gather.2.cloned.1.call-done) | copy-start | bytes 18874372
Sparse Core Ops, SparseCore 0:
  83.5 139.1 all-gather.1
  275.7 59.1 reduce-scatter.1
